TPU v7x, 32 devices: a whole 2x2x4 slice. The times are simulated.
32 devices in a mesh: dev: 32 (over z, y, x, core).
Axes of the slice: x: 2, y: 2, z: 4, core: 2. Of those that a mesh axis runs over, the one named last changes fastest.
Arguments:
- grain_boxes: float32 [64, 64, 4096], P('dev'), may hold values from 0 to 1
- box_anchors: int32 [64, 3], P('dev'), may hold values from 0 to 31, as said below
- migrations: int32 [32, 2], P('dev'), may hold values from 0 to 1, as said below
Outputs:
- new_boxes: float32 [64, 64, 4096], P('dev')
Inputs may be any that keep to these rules, and one draw needn't show every extreme that they name: `box_anchors`: box b belongs to device d = b // 2; its first coordinate is d - 1, d or d + 1 modulo 32; the other two coordinates are 0 to 3. `migrations`: the two entries of a row differ, so each device hands exactly one box to each neighbour and receives one from each.
All inputs are finite; a program needn't handle non-finite values.
Results may differ from a plain program's by a relative error of at most 0.0003.
Values sent between devices are 32-bit elements; how exact they have to be, the bound alone decides.
A program may use at most 128 MiB of HBM per device.

v0:
```python
import functools

import jax
import jax.numpy as jnp
from jax import lax
from jax.experimental import pallas as pl
from jax.experimental.pallas import tpu as pltpu
from jax.sharding import PartitionSpec as P


SUBSTEPS = 4

growth_rate = 1.0
quartic_rate = 1.0
coupling = 1.5
gradient_energy = 2.0
time_step = 0.02

LANES = 128


def from_outward(value, steps):
    count = lax.axis_size("dev")
    pairs = []
    for target in range(count):
        outward = 1 if target % 2 else -1
        pairs.append(((target + outward * steps) % count, target))
    return lax.ppermute(value, "dev", pairs)


def offsets_of(source, target, grid_tiles, skip=None):
    delta_x = lax.rem(source[0] - target[0] + grid_tiles + grid_tiles // 2, grid_tiles)
    delta_x = delta_x - grid_tiles // 2
    delta_y = lax.rem(source[1] - target[1] + 4, 4)
    delta_z = lax.rem(source[2] - target[2] + 4, 4)
    meets = (delta_x >= -1) & (delta_x <= 1) & (delta_y != 2) & (delta_z != 2)
    if skip is not None:
        meets = meets & jnp.logical_not(skip)
    return meets, delta_x, delta_y, delta_z


def add_squares(total_ref, box_ref, offsets, halves=(0, 1), ready=None):
    half = box_ref.shape[0] // 2
    area_half = box_ref.shape[1] // 2
    edge = 2 * half
    meets, delta_x, delta_y, delta_z = offsets

    @pl.when(meets)
    def _():
        if ready is not None:
            ready()
        lane = lax.broadcasted_iota(jnp.int32, (half, LANES), 1) % edge
        first = jnp.where(delta_z == 1, half, 0)
        final = jnp.where(delta_z == 3, half, edge)
        inside = (lane >= first) & (lane < final)
        shift = delta_z * half
        for half_x in halves:
            from_x = half_x - delta_x
            row_out = (half_x - halves[0]) * half
            for half_y in range(2):
                from_y = lax.rem(half_y - delta_y + 4, 4)

                @pl.when((from_x >= 0) & (from_x <= 1) & (from_y <= 1))
                def _():
                    row = pl.multiple_of(from_x * half, half)

                    def chunk(at, carry):
                        column = pl.multiple_of(from_y * area_half + at * LANES, LANES)
                        out = half_y * (area_half // LANES) + at
                        value = box_ref[pl.ds(row, half), pl.ds(column, LANES)]
                        value = pltpu.roll(value * value, shift, 1)
                        value = jnp.where(inside, value, 0.0)
                        total_ref[out, row_out : row_out + half, :] += value
                        return carry

                    lax.fori_loop(0, area_half // LANES, chunk, 0, unroll=4)


def box_anchor(meta_ref, row, slot):
    return [meta_ref[row, slot * 3 + axis] for axis in range(3)]


def target_slots(meta_ref, row):
    outward = meta_ref[0, 8]
    right = (outward == 1) == (row == 1)
    slot = jnp.where(right, meta_ref[row, 6], meta_ref[row, 7])
    out_slot = jnp.where(right, meta_ref[0, 6], meta_ref[0, 7])
    return slot, out_slot


def early_kernel(grid_tiles, meta_ref, own_ref, partner_ref, full_ref, near_ref, outer_ref, inner_ref):
    outward = meta_ref[0, 8]
    slot_full = jnp.where(outward == 1, meta_ref[3, 6], meta_ref[3, 7])
    slot_near = jnp.where(outward == 1, meta_ref[4, 6], meta_ref[4, 7])
    target_full = box_anchor(meta_ref, 3, slot_full)
    target_near = box_anchor(meta_ref, 4, slot_near)
    slot_outer = target_slots(meta_ref, 2)[0]
    slot_inner = target_slots(meta_ref, 1)[0]
    target_outer = box_anchor(meta_ref, 2, slot_outer)
    target_inner = box_anchor(meta_ref, 1, slot_inner)
    for total_ref in (full_ref, near_ref, outer_ref, inner_ref):
        total_ref[...] = jnp.zeros_like(total_ref)
    for row, refs in ((0, own_ref), (1, partner_ref)):

        def one_box(box, carry, row=row, refs=refs):
            anchor = box_anchor(meta_ref, row, box)
            box_ref = refs.at[box]
            skip = box == slot_inner if row == 1 else None
            add_squares(full_ref, box_ref, offsets_of(anchor, target_full, grid_tiles))
            add_squares(outer_ref, box_ref, offsets_of(anchor, target_outer, grid_tiles))
            add_squares(inner_ref, box_ref, offsets_of(anchor, target_inner, grid_tiles, skip))
            if row == 0:
                near = offsets_of(anchor, target_near, grid_tiles)
                for side in range(2):

                    @pl.when(outward == 1 - side)
                    def _(side=side):
                        add_squares(near_ref, box_ref, near, halves=(side,))

            return carry

        lax.fori_loop(0, 2, one_box, 0)


def relax_into(order_refs, factor_ref, out_ref, edge):
    chunks, rows, _ = factor_ref.shape
    groups = rows // 8
    lane = lax.broadcasted_iota(jnp.int32, (rows, LANES), 1)
    row = lax.broadcasted_iota(jnp.int32, (8, LANES), 0)
    low_half = lane < edge
    at_z_end = lane % edge == edge - 1
    at_z_start = lane % edge == 0
    for substep in range(SUBSTEPS):
        source = order_refs[substep % 2]
        target = order_refs[(substep + 1) % 2]
        final = substep == SUBSTEPS - 1

        def chunk(at, carry, source=source, target=target, final=final):
            swapped_before, swapped, order = carry
            after = source[at + 2]
            swapped_after = pltpu.roll(after, edge, 1)
            factor = factor_ref[at]
            beside = jnp.where(low_half, swapped, swapped_after)
            beside += jnp.where(low_half, swapped_before, swapped)
            beside += jnp.where(at_z_end, 0.0, pltpu.roll(order, LANES - 1, 1))
            beside += jnp.where(at_z_start, 0.0, pltpu.roll(order, 1, 1))
            upper = jnp.where(row == 7, 0.0, pltpu.roll(order[:8], 7, 0))
            lower = jnp.where(row == 0, 0.0, pltpu.roll(order[rows - 8 :], 1, 0))
            beside += jnp.concatenate([order[8:], upper], axis=0)
            beside += jnp.concatenate([lower, order[: rows - 8]], axis=0)
            relaxed = order * (factor - (time_step * quartic_rate) * (order * order))
            relaxed += (time_step * gradient_energy) * beside
            if final:
                for group in range(groups):
                    picked = pl.ds(group, groups, stride=groups)
                    out_ref.at[at][picked, :] = relaxed[group * 8 : group * 8 + 8]
            else:
                target[at + 1] = relaxed
            return swapped, swapped_after, after

        first = source[1]
        zeros = jnp.zeros((rows, LANES), jnp.float32)
        lax.fori_loop(0, chunks, chunk, (zeros, pltpu.roll(first, edge, 1), first), unroll=2)


def relax_kernel(grid_tiles, target_row, source_rows, aliased, *refs):
    meta_ref, total_in_ref, part_ref, target_ref = refs[:4]
    count = len(source_rows)
    source_refs = refs[4 : 4 + count]
    out_ref, order_a, order_b, total_ref, result_ref, stage, target_stage, sems = refs[
        4 + count + aliased :
    ]
    chunks, rows, _ = total_ref.shape
    half = rows // 2
    groups = rows // 8
    slot, out_slot = target_slots(meta_ref, target_row)
    target = box_anchor(meta_ref, target_row, slot)

    def fetch(at, carry):
        columns = pl.ds(pl.multiple_of(at * LANES, LANES), LANES)
        pltpu.make_async_copy(
            target_ref.at[slot, :, columns], target_stage.at[at], sems.at[2 * count]
        ).start()
        return carry

    lax.fori_loop(0, chunks, fetch, 0)
    work = []
    for place, source_row in enumerate(source_rows):
        for box in range(2):
            source = box_anchor(meta_ref, source_row, box)
            skip = slot == box if source_row == target_row else None
            offsets = offsets_of(source, target, grid_tiles, skip)
            at = 2 * place + box
            copy = pltpu.make_async_copy(source_refs[place].at[box], stage.at[at], sems.at[at])
            pl.when(offsets[0])(copy.start)
            work.append((at, offsets, copy))
    for order_ref in (order_a, order_b):
        order_ref[0] = jnp.zeros((rows, LANES), jnp.float32)
        order_ref[chunks + 1] = jnp.zeros((rows, LANES), jnp.float32)
    if target_row == 2:
        total_ref[...] = total_in_ref[...] + part_ref[...]
    else:
        total_ref[...] = total_in_ref[...]
        near_row = pl.multiple_of((1 - meta_ref[0, 8]) * half, half)
        total_ref[:, pl.ds(near_row, half), :] += part_ref[...]
    for at, offsets, copy in work:
        add_squares(total_ref, stage.at[at], offsets, ready=copy.wait)
    pltpu.make_async_copy(target_stage, target_stage, sems.at[2 * count]).wait()
    base = 1.0 + time_step * (growth_rate - 6.0 * gradient_energy)
    factor_ref = result_ref

    def prepare(at, carry):
        for group in range(groups):
            picked = pl.ds(group, groups, stride=groups)
            into = pl.ds(group * 8, 8)
            order_a[at + 1, into, :] = target_stage.at[at][picked, :]
            factor_ref[at, into, :] = (
                base - (time_step * 2.0 * coupling) * total_ref.at[at][picked, :]
            )
        return carry

    lax.fori_loop(0, chunks, prepare, 0, unroll=2)
    relax_into((order_a, order_b), factor_ref, total_ref, rows)

    def deliver(at, carry):
        columns = pl.ds(pl.multiple_of(at * LANES, LANES), LANES)
        pltpu.make_async_copy(
            total_ref.at[at], out_ref.at[out_slot, :, columns], sems.at[2 * count]
        ).start()
        return carry

    lax.fori_loop(0, chunks, deliver, 0)
    pltpu.make_async_copy(total_ref, total_ref, sems.at[2 * count]).wait()


def on_device(grain_boxes, box_anchors, migrations):
    _, box_edge, area = grain_boxes.shape
    devices = lax.axis_size("dev")
    position = lax.axis_index("dev")
    outward = (position % 2).astype(jnp.int32).reshape(1, 1)
    meta = jnp.concatenate([box_anchors.reshape(1, -1), migrations.reshape(1, -1)], axis=1)
    outer = from_outward(grain_boxes, 1)
    partner = from_outward(grain_boxes, -1)
    metas = [meta] + [from_outward(meta, steps) for steps in (-1, 1, 2, 3, -2, -3)]
    metas = jnp.concatenate(metas, axis=0)
    metas = jnp.concatenate([metas, jnp.broadcast_to(outward, (metas.shape[0], 1))], axis=1)

    smem = pl.BlockSpec(memory_space=pltpu.SMEM)
    vmem = pl.BlockSpec(memory_space=pltpu.VMEM)
    anywhere = pl.BlockSpec(memory_space=pl.ANY)
    chunks = area // LANES
    half_shape = jax.ShapeDtypeStruct((chunks, box_edge // 2, LANES), jnp.float32)
    box_shape = jax.ShapeDtypeStruct((chunks, box_edge, LANES), jnp.float32)
    full_part, near_part, outer_sum, inner_sum = pl.pallas_call(
        functools.partial(early_kernel, devices),
        out_shape=(box_shape, half_shape, box_shape, box_shape),
        in_specs=[smem, vmem, vmem],
        out_specs=(vmem,) * 4,
        name="early_sums",
        cost_estimate=pl.CostEstimate(flops=8_000_000, bytes_accessed=8_000_000, transcendentals=0),
    )(metas, grain_boxes, partner)
    full_sum = from_outward(full_part, 3)
    near_sum = from_outward(near_part, -4)
    later_boxes, outer = lax.optimization_barrier((grain_boxes, outer))
    outer2 = from_outward(later_boxes, 2)
    inner2 = from_outward(outer, -1)
    inner3 = from_outward(outer2, -1)

    def relax(target_row, source_rows, total, part, target_boxes, sources, before):
        count = len(source_rows)
        aliased = 0 if before is None else 1
        box_scratch = pltpu.VMEM((chunks, box_edge, LANES), jnp.float32)
        padded = pltpu.VMEM((chunks + 2, box_edge, LANES), jnp.float32)
        extra = () if before is None else (before,)
        return pl.pallas_call(
            functools.partial(relax_kernel, devices, target_row, source_rows, aliased),
            out_shape=jax.ShapeDtypeStruct(grain_boxes.shape, jnp.float32),
            in_specs=[smem, vmem, vmem] + [anywhere] * (1 + count + aliased),
            out_specs=anywhere,
            input_output_aliases={4 + count: 0} if aliased else {},
            scratch_shapes=[
                padded,
                padded,
                box_scratch,
                box_scratch,
                pltpu.VMEM((2 * count, box_edge, area), jnp.float32),
                box_scratch,
                pltpu.SemaphoreType.DMA((2 * count + 1,)),
            ],
            name="relax_outer" if target_row == 2 else "relax_inner",
            compiler_params=pltpu.CompilerParams(vmem_limit_bytes=32 * 1024 * 1024),
            cost_estimate=pl.CostEstimate(
                flops=20_000_000, bytes_accessed=10_000_000, transcendentals=0
            ),
        )(metas, total, part, target_boxes, *sources, *extra)

    first = relax(2, (2, 5, 3), outer_sum, full_sum, outer, (outer, inner2, outer2), None)
    return relax(
        1, (2, 5, 3, 6), inner_sum, near_sum, partner, (outer, inner2, outer2, inner3), first
    )


def solution(mesh):
    in_specs = (P("dev", None, None), P("dev", None), P("dev", None))
    out_specs = P("dev", None, None)
    return jax.shard_map(
        on_device, mesh=mesh, in_specs=in_specs, out_specs=out_specs, check_vma=False
    )
```

profile of v0, /device:TPU:1, one launch (start us, length us, event | category | flops | bytes accessed | tf_op | source)
XLA Modules:
  0.0 180.9 jit_solution(2854374399918897691)
XLA Ops:
  0.0 2.6 %collective-permute-start.8 = (f32[2,64,4096]{2,1,0:T(8,128)}, f32[2,64,4096]{2,1,0:T(8,128)S(1)}, u32[]{:S(2)}, u32[]{:S(2)}) collective-permute-start(f32[2,64,4096]{2,1,0:T(8,128)} %own_ref.1), channel_id=1, source_target_pairs={{31,0},{2,1},{1,2},{4,3},{3,4},{6,5},{5,6},{8,7},{7,8},{10,9},{9,1... | collective-permute-start | bytes 6291464 | tf_op jit(solution)/shard_map/ppermute | solution.py:28
  2.6 45.8 %collective-permute-done.8.refs_3_.refs_4_ = f32[2,64,4096]{2,1,0:T(8,128)S(1)} collective-permute-done((f32[2,64,4096]{2,1,0:T(8,128)}, f32[2,64,4096]{2,1,0:T(8,128)S(1)}, u32[]{:S(2)}, u32[]{:S(2)}) %collective-permute-start.8) | collective-permute-done | bytes 2097184 | tf_op jit(solution)/shard_map/ppermute | solution.py:28
  48.4 0.0 collective-permute-start.10
  48.4 2.8 %collective-permute-start.6 = (f32[2,64,4096]{2,1,0:T(8,128)}, f32[2,64,4096]{2,1,0:T(8,128)}, u32[]{:S(2)}, u32[]{:S(2)}) collective-permute-start(f32[2,64,4096]{2,1,0:T(8,128)} %own_ref.1), channel_id=1, source_target_pairs={{1,0},{0,1},{3,2},{2,3},{5,4},{4,5},{7,6},{6,7},{9,8},{8,9},{11,10... | collective-permute-start | bytes 6291464 | tf_op jit(solution)/shard_map/ppermute | solution.py:28
  51.1 0.0 collective-permute-start.9
  51.1 44.6 %collective-permute-done.10.refs_6_ = f32[2,64,4096]{2,1,0:T(8,128)} collective-permute-done((f32[2,64,4096]{2,1,0:T(8,128)}, f32[2,64,4096]{2,1,0:T(8,128)}, u32[]{:S(2)}, u32[]{:S(2)}) %collective-permute-start.10) | collective-permute-done | bytes 2097184 | tf_op jit(solution)/shard_map/ppermute | solution.py:28
  95.8 0.0 collective-permute-start.11
  95.8 0.8 reshape.7
  96.5 0.7 pad_add_fusion
  97.3 7.4 %collective-permute-start.5 = (s32[1,8]{1,0:T(1,128)S(1)}, s32[1,8]{1,0:T(1,128)S(1)}, u32[]{:S(2)}, u32[]{:S(2)}) collective-permute-start(s32[1,8]{1,0:T(1,128)S(1)} %pad_add_fusion), channel_id=1, source_target_pairs={{3,0},{30,1},{5,2},{0,3},{7,4},{2,5},{9,6},{4,7},{11,8},{6,9},{13,... | collective-permute-start | bytes 104 | tf_op jit(solution)/shard_map/ppermute | solution.py:28
  104.7 0.0 collective-permute-start.4
  104.7 1.2 collective-permute-done.5
  106.0 0.0 collective-permute-start.3
  106.0 4.8 %collective-permute-done.4 = s32[1,8]{1,0:T(1,128)S(1)} collective-permute-done((s32[1,8]{1,0:T(1,128)S(1)}, s32[1,8]{1,0:T(1,128)S(1)}, u32[]{:S(2)}, u32[]{:S(2)}) %collective-permute-start.4) | collective-permute-done | bytes 64 | tf_op jit(solution)/shard_map/ppermute | solution.py:28
  110.7 0.0 collective-permute-start.2
  110.7 0.0 collective-permute-done.3
  110.7 0.9 collective-permute-start.1
  111.6 1.5 collective-permute-done.2
  113.1 2.7 %collective-permute-start = (s32[1,8]{1,0:T(1,128)S(1)}, s32[1,8]{1,0:T(1,128)S(1)}, u32[]{:S(2)}, u32[]{:S(2)}) collective-permute-start(s32[1,8]{1,0:T(1,128)S(1)} %pad_add_fusion), channel_id=1, source_target_pairs={{1,0},{0,1},{3,2},{2,3},{5,4},{4,5},{7,6},{6,7},{9,8},{8,9},{11,10... | collective-permute-start | bytes 104 | tf_op jit(solution)/shard_map/ppermute | solution.py:28
  115.9 0.0 collective-permute-done.1
  115.9 0.8 collective-permute-done
  116.7 0.6 concatenate.11.meta_ref.refs_0_
  117.3 0.0 collective-permute-done.6.partner_ref.refs_3_
  117.3 6.4 %early_sums.1 = (f32[32,64,128]{2,1,0:T(8,128)}, f32[32,32,128]{2,1,0:T(8,128)}, f32[32,64,128]{2,1,0:T(8,128)}, f32[32,64,128]{2,1,0:T(8,128)}) custom-call(s32[7,9]{1,0:T(8,128)} %concatenate.11.meta_ref.refs_0_, f32[2,64,4096]{2,1,0:T(8,128)} %own_ref.1, f32[2,64,4096]{2,1,0:T(8,128)} %collective-permute-done.6.partner_ref.refs_3_), custom_call_target="tpu_custom_call" | custom-call | flops 8000000 | bytes 8000000 | tf_op jit(solution)/shard_map/early_sums/pallas_call | solution.py:254
  123.7 0.0 collective-permute-start.12
  123.7 31.3 %collective-permute-done.12.refs_2_ = f32[32,64,128]{2,1,0:T(8,128)S(1)} collective-permute-done((f32[32,64,128]{2,1,0:T(8,128)}, f32[32,64,128]{2,1,0:T(8,128)S(1)}, u32[]{:S(2)}, u32[]{:S(2)}) %collective-permute-start.12) | collective-permute-done | bytes 1048608 | tf_op jit(solution)/shard_map/ppermute | solution.py:28
  155.0 0.0 collective-permute-done.9.refs_5_
  155.0 1.2 copy-done.1
  156.3 11.1 %relax_outer.1.refs_8_ = f32[2,64,4096]{2,1,0:T(8,128)} custom-call(s32[7,9]{1,0:T(8,128)S(1)} %copy-done.2, f32[32,64,128]{2,1,0:T(8,128)S(1)} %copy-done.1, f32[32,64,128]{2,1,0:T(8,128)S(1)} %collective-permute-done.12.refs_2_, f32[2,64,4096]{2,1,0:T(8,128)S(1)} %collective-permute-done.8.refs_3_.refs_4_, ...), custom_call_target="tpu_custom_call" | custom-call | flops 20000000 | bytes 10000000 | tf_op jit(solution)/shard_map/relax_outer/pallas_call | solution.py:275
  167.4 0.0 collective-permute-done.7.refs_2_
  167.4 0.0 collective-permute-done.11.refs_7_
  167.4 13.4 %relax_inner.1 = f32[2,64,4096]{2,1,0:T(8,128)} custom-call(s32[7,9]{1,0:T(8,128)S(1)} %copy-done.2, f32[32,64,128]{2,1,0:T(8,128)S(1)} %copy-done, f32[32,32,128]{2,1,0:T(8,128)S(1)} %collective-permute-done.7.refs_2_, f32[2,64,4096]{2,1,0:T(8,128)} %collective-permute-done.6.partner_ref.refs_3_, ...), custom_call_target="tpu_custom_call", output_to_operand_aliasing={{}: (8, {})} | custom-call | flops 20000000 | bytes 10000000 | tf_op jit(solution)/shard_map/relax_inner/pallas_call | solution.py:275
  (7 shorter events, 0.0 us)
Async XLA Ops:
  0.0 48.4 %collective-permute-start.8 = (f32[2,64,4096]{2,1,0:T(8,128)}, f32[2,64,4096]{2,1,0:T(8,128)S(1)}, u32[]{:S(2)}, u32[]{:S(2)}) collective-permute-start(f32[2,64,4096]{2,1,0:T(8,128)} %own_ref.1), channel_id=1, source_target_pairs={{31,0},{2,1},{1,2},{4,3},{3,4},{6,5},{5,6},{8,7},{7,8},{10,9},{9,1... | collective-permute-start | bytes 6291464 | tf_op jit(solution)/shard_map/ppermute | solution.py:28
  48.4 47.4 %collective-permute-start.10 = (f32[2,64,4096]{2,1,0:T(8,128)}, f32[2,64,4096]{2,1,0:T(8,128)}, u32[]{:S(2)}, u32[]{:S(2)}) collective-permute-start(f32[2,64,4096]{2,1,0:T(8,128)} %own_ref.1), channel_id=1, source_target_pairs={{30,0},{3,1},{0,2},{5,3},{2,4},{7,5},{4,6},{9,7},{6,8},{11,9},{8,1... | collective-permute-start | bytes 6291464 | tf_op jit(solution)/shard_map/ppermute | solution.py:28
  48.4 68.9 %collective-permute-start.6 = (f32[2,64,4096]{2,1,0:T(8,128)}, f32[2,64,4096]{2,1,0:T(8,128)}, u32[]{:S(2)}, u32[]{:S(2)}) collective-permute-start(f32[2,64,4096]{2,1,0:T(8,128)} %own_ref.1), channel_id=1, source_target_pairs={{1,0},{0,1},{3,2},{2,3},{5,4},{4,5},{7,6},{6,7},{9,8},{8,9},{11,10... | collective-permute-start | bytes 6291464 | tf_op jit(solution)/shard_map/ppermute | solution.py:28
  51.1 103.9 %collective-permute-start.9 = (f32[2,64,4096]{2,1,0:T(8,128)S(1)}, f32[2,64,4096]{2,1,0:T(8,128)}, u32[]{:S(2)}, u32[]{:S(2)}) collective-permute-start(f32[2,64,4096]{2,1,0:T(8,128)S(1)} %collective-permute-done.8.refs_3_.refs_4_), channel_id=1, source_target_pairs={{1,0},{0,1},{3,2},{2,3},{5,4},{4,5},{7,6},{6,7},{9,8},{8,9},{11,10... | collective-permute-start | bytes 6291464 | tf_op jit(solution)/shard_map/ppermute | solution.py:28
  95.8 71.7 %collective-permute-start.11 = (f32[2,64,4096]{2,1,0:T(8,128)}, f32[2,64,4096]{2,1,0:T(8,128)}, u32[]{:S(2)}, u32[]{:S(2)}) collective-permute-start(f32[2,64,4096]{2,1,0:T(8,128)} %collective-permute-done.10.refs_6_), channel_id=1, source_target_pairs={{1,0},{0,1},{3,2},{2,3},{5,4},{4,5},{7,6},{6,7},{9,8},{8,9},{11,10... | collective-permute-start | bytes 6291464 | tf_op jit(solution)/shard_map/ppermute | solution.py:28
  97.3 8.7 %collective-permute-start.5 = (s32[1,8]{1,0:T(1,128)S(1)}, s32[1,8]{1,0:T(1,128)S(1)}, u32[]{:S(2)}, u32[]{:S(2)}) collective-permute-start(s32[1,8]{1,0:T(1,128)S(1)} %pad_add_fusion), channel_id=1, source_target_pairs={{3,0},{30,1},{5,2},{0,3},{7,4},{2,5},{9,6},{4,7},{11,8},{6,9},{13,... | collective-permute-start | bytes 104 | tf_op jit(solution)/shard_map/ppermute | solution.py:28
  104.7 6.0 %collective-permute-start.4 = (s32[1,8]{1,0:T(1,128)S(1)}, s32[1,8]{1,0:T(1,128)S(1)}, u32[]{:S(2)}, u32[]{:S(2)}) collective-permute-start(s32[1,8]{1,0:T(1,128)S(1)} %pad_add_fusion), channel_id=1, source_target_pairs={{2,0},{31,1},{4,2},{1,3},{6,4},{3,5},{8,6},{5,7},{10,8},{7,9},{12,... | collective-permute-start | bytes 104 | tf_op jit(solution)/shard_map/ppermute | solution.py:28
  106.0 4.8 %collective-permute-start.3 = (s32[1,8]{1,0:T(1,128)S(1)}, s32[1,8]{1,0:T(1,128)S(1)}, u32[]{:S(2)}, u32[]{:S(2)}) collective-permute-start(s32[1,8]{1,0:T(1,128)S(1)} %pad_add_fusion), channel_id=1, source_target_pairs={{29,0},{4,1},{31,2},{6,3},{1,4},{8,5},{3,6},{10,7},{5,8},{12,9},{7... | collective-permute-start | bytes 104 | tf_op jit(solution)/shard_map/ppermute | solution.py:28
  110.7 2.4 %collective-permute-start.2 = (s32[1,8]{1,0:T(1,128)S(1)}, s32[1,8]{1,0:T(1,128)S(1)}, u32[]{:S(2)}, u32[]{:S(2)}) collective-permute-start(s32[1,8]{1,0:T(1,128)S(1)} %pad_add_fusion), channel_id=1, source_target_pairs={{30,0},{3,1},{0,2},{5,3},{2,4},{7,5},{4,6},{9,7},{6,8},{11,9},{8,1... | collective-permute-start | bytes 104 | tf_op jit(solution)/shard_map/ppermute | solution.py:28
  110.7 5.1 %collective-permute-start.1 = (s32[1,8]{1,0:T(1,128)S(1)}, s32[1,8]{1,0:T(1,128)S(1)}, u32[]{:S(2)}, u32[]{:S(2)}) collective-permute-start(s32[1,8]{1,0:T(1,128)S(1)} %pad_add_fusion), channel_id=1, source_target_pairs={{31,0},{2,1},{1,2},{4,3},{3,4},{6,5},{5,6},{8,7},{7,8},{10,9},{9,1... | collective-permute-start | bytes 104 | tf_op jit(solution)/shard_map/ppermute | solution.py:28
  113.1 3.5 %collective-permute-start = (s32[1,8]{1,0:T(1,128)S(1)}, s32[1,8]{1,0:T(1,128)S(1)}, u32[]{:S(2)}, u32[]{:S(2)}) collective-permute-start(s32[1,8]{1,0:T(1,128)S(1)} %pad_add_fusion), channel_id=1, source_target_pairs={{1,0},{0,1},{3,2},{2,3},{5,4},{4,5},{7,6},{6,7},{9,8},{8,9},{11,10... | collective-permute-start | bytes 104 | tf_op jit(solution)/shard_map/ppermute | solution.py:28
  117.3 37.7 %copy-start.2 = (s32[7,9]{1,0:T(8,128)S(1)}, s32[7,9]{1,0:T(8,128)}, u32[]{:S(2)}) copy-start(s32[7,9]{1,0:T(8,128)} %concatenate.11.meta_ref.refs_0_) | copy-start | bytes 760
  123.7 31.3 %collective-permute-start.12 = (f32[32,64,128]{2,1,0:T(8,128)}, f32[32,64,128]{2,1,0:T(8,128)S(1)}, u32[]{:S(2)}, u32[]{:S(2)}) collective-permute-start(f32[32,64,128]{2,1,0:T(8,128)} %get-tuple-element.16), channel_id=1, source_target_pairs={{29,0},{4,1},{31,2},{6,3},{1,4},{8,5},{3,6},{10,7},{5,8},{12,9},{7... | collective-permute-start | bytes 3145736 | tf_op jit(solution)/shard_map/ppermute | solution.py:28
  123.7 43.7 %collective-permute-start.7 = (f32[32,32,128]{2,1,0:T(8,128)}, f32[32,32,128]{2,1,0:T(8,128)S(1)}, u32[]{:S(2)}, u32[]{:S(2)}) collective-permute-start(f32[32,32,128]{2,1,0:T(8,128)} %get-tuple-element.12), channel_id=1, source_target_pairs={{4,0},{29,1},{6,2},{31,3},{8,4},{1,5},{10,6},{3,7},{12,8},{5,9},{1... | collective-permute-start | bytes 1572872 | tf_op jit(solution)/shard_map/ppermute | solution.py:28
  155.0 1.2 copy-start.1
  156.3 11.2 %copy-start = (f32[32,64,128]{2,1,0:T(8,128)S(1)}, f32[32,64,128]{2,1,0:T(8,128)}, u32[]{:S(2)}) copy-start(f32[32,64,128]{2,1,0:T(8,128)} %get-tuple-element.11.refs_1_) | copy-start | bytes 3145732
where the time goes:
time: 181 us
  waiting for transfers between devices  130 us (72%)
  Pallas kernels  31 us (17%)
  starting transfers between devices  16.5 us (9%)
  local copies, waits for them, and re-layouts  2.62 us (1%)
    ppermute x13, waiting for transfers between devices, from_outward(): return lax.ppermute(value, 'dev', pairs)  130 us
    pallas_call x2, Pallas kernels, relax(): pl.pallas_call(functools.partial(relax_kernel, devices, target_row, sourc...  24.6 us
    ppermute x13, starting transfers between devices, from_outward(): return lax.ppermute(value, 'dev', pairs)  16.5 us
    pallas_call x1, Pallas kernels, on_device(): pl.pallas_call(functools.partial(early_kernel, devices), out_shape=(box_s...  6.43 us
  transfers between devices with their start and end apart: 13, of which 7 were waited for; matrix products, arithmetic and copies ran while one was open for 1% of the time, Pallas kernels for 10%

commit v1 on v0

--- a/solution.py
+++ b/solution.py
@@ -239,11 +239,20 @@
     position = lax.axis_index("dev")
     outward = (position % 2).astype(jnp.int32).reshape(1, 1)
     meta = jnp.concatenate([box_anchors.reshape(1, -1), migrations.reshape(1, -1)], axis=1)
+    metas = [meta]
+    for steps in (-1, 1, 2, 3):
+        metas.append(from_outward(meta, steps))
+    metas.append(from_outward(jnp.concatenate(metas[2:4], axis=0), -1))
+    partner = from_outward(grain_boxes, -1)
     outer = from_outward(grain_boxes, 1)
-    partner = from_outward(grain_boxes, -1)
-    metas = [meta] + [from_outward(meta, steps) for steps in (-1, 1, 2, 3, -2, -3)]
-    metas = jnp.concatenate(metas, axis=0)
-    metas = jnp.concatenate([metas, jnp.broadcast_to(outward, (metas.shape[0], 1))], axis=1)
+    outer2 = from_outward(grain_boxes, 2)
+
+    def with_flag(rows):
+        rows = jnp.concatenate(rows, axis=0)
+        return jnp.concatenate([rows, jnp.broadcast_to(outward, (rows.shape[0], 1))], axis=1)
+
+    early_metas = with_flag(metas[:5])
+    metas = with_flag(metas)
 
     smem = pl.BlockSpec(memory_space=pltpu.SMEM)
     vmem = pl.BlockSpec(memory_space=pltpu.VMEM)
@@ -258,11 +267,9 @@
         out_specs=(vmem,) * 4,
         name="early_sums",
         cost_estimate=pl.CostEstimate(flops=8_000_000, bytes_accessed=8_000_000, transcendentals=0),
-    )(metas, grain_boxes, partner)
+    )(early_metas, grain_boxes, partner)
     full_sum = from_outward(full_part, 3)
     near_sum = from_outward(near_part, -4)
-    later_boxes, outer = lax.optimization_barrier((grain_boxes, outer))
-    outer2 = from_outward(later_boxes, 2)
     inner2 = from_outward(outer, -1)
     inner3 = from_outward(outer2, -1)
 

time: 181 us -> 173 us (0.956)
  waiting for transfers between devices: 130 us -> 118 us
  starting transfers between devices: 16.5 us -> 19.8 us
    ppermute x13 -> x12, waiting for transfers between devices: 130 us -> 118 us  [from_outward(): return lax.ppermute(value, 'dev', pairs)]
    ppermute x13 -> x12, starting transfers between devices: 16.5 us -> 19.8 us  [from_outward(): return lax.ppermute(value, 'dev', pairs)]
  transfers between devices with their start and end apart: 13 -> 12, of which waited for: 7 -> 5; matrix products, arithmetic and copies ran while one was open for 1% -> 1% of each run, Pallas kernels for 10% -> 10%
where the time goes in v1:
time: 173 us
  waiting for transfers between devices  118 us (68%)
  Pallas kernels  31.6 us (18%)
  starting transfers between devices  19.8 us (11%)
  local copies, waits for them, and re-layouts  2.64 us (2%)
    ppermute x12, waiting for transfers between devices, from_outward(): return lax.ppermute(value, 'dev', pairs)  118 us
    pallas_call x2, Pallas kernels, relax(): pl.pallas_call(functools.partial(relax_kernel, devices, target_row, sourc...  25.2 us
    ppermute x12, starting transfers between devices, from_outward(): return lax.ppermute(value, 'dev', pairs)  19.8 us
    pallas_call x1, Pallas kernels, on_device(): pl.pallas_call(functools.partial(early_kernel, devices), out_shape=(box_s...  6.41 us
  transfers between devices with their start and end apart: 12, of which 5 were waited for; matrix products, arithmetic and copies ran while one was open for 1% of the time, Pallas kernels for 10%

profile of v1, /device:TPU:1, one launch (start us, length us, event | category | flops | bytes accessed | tf_op | source)
XLA Modules:
  0.0 173.0 jit_solution(16685882576055265672)
XLA Ops:
  0.0 2.6 %collective-permute-start.7 = (f32[2,64,4096]{2,1,0:T(8,128)}, f32[2,64,4096]{2,1,0:T(8,128)S(1)}, u32[]{:S(2)}, u32[]{:S(2)}) collective-permute-start(f32[2,64,4096]{2,1,0:T(8,128)} %own_ref.1), channel_id=1, source_target_pairs={{31,0},{2,1},{1,2},{4,3},{3,4},{6,5},{5,6},{8,7},{7,8},{10,9},{9,1... | collective-permute-start | bytes 6291464 | tf_op jit(solution)/shard_map/ppermute | solution.py:28
  2.6 3.4 %collective-permute-start.9 = (f32[2,64,4096]{2,1,0:T(8,128)}, f32[2,64,4096]{2,1,0:T(8,128)}, u32[]{:S(2)}, u32[]{:S(2)}) collective-permute-start(f32[2,64,4096]{2,1,0:T(8,128)} %own_ref.1), channel_id=1, source_target_pairs={{30,0},{3,1},{0,2},{5,3},{2,4},{7,5},{4,6},{9,7},{6,8},{11,9},{8,1... | collective-permute-start | bytes 6291464 | tf_op jit(solution)/shard_map/ppermute | solution.py:28
  6.0 0.4 collective-permute-start.5
  6.4 84.9 %collective-permute-done.7.refs_3_.refs_4_ = f32[2,64,4096]{2,1,0:T(8,128)S(1)} collective-permute-done((f32[2,64,4096]{2,1,0:T(8,128)}, f32[2,64,4096]{2,1,0:T(8,128)S(1)}, u32[]{:S(2)}, u32[]{:S(2)}) %collective-permute-start.7) | collective-permute-done | bytes 2097184 | tf_op jit(solution)/shard_map/ppermute | solution.py:28
  91.3 0.0 collective-permute-start.8
  91.3 2.7 %collective-permute-done.9.refs_6_ = f32[2,64,4096]{2,1,0:T(8,128)} collective-permute-done((f32[2,64,4096]{2,1,0:T(8,128)}, f32[2,64,4096]{2,1,0:T(8,128)}, u32[]{:S(2)}, u32[]{:S(2)}) %collective-permute-start.9) | collective-permute-done | bytes 2097184 | tf_op jit(solution)/shard_map/ppermute | solution.py:28
  94.0 0.0 collective-permute-start.10
  94.0 0.8 reshape.10
  94.8 0.7 pad_add_fusion.1
  95.5 1.6 collective-permute-start.3
  97.2 4.7 %collective-permute-start.2 = (s32[1,8]{1,0:T(1,128)S(1)}, s32[1,8]{1,0:T(1,128)S(1)}, u32[]{:S(2)}, u32[]{:S(2)}) collective-permute-start(s32[1,8]{1,0:T(1,128)S(1)} %pad_add_fusion.1), channel_id=1, source_target_pairs={{30,0},{3,1},{0,2},{5,3},{2,4},{7,5},{4,6},{9,7},{6,8},{11,9},{8,1... | collective-permute-start | bytes 104 | tf_op jit(solution)/shard_map/ppermute | solution.py:28
  101.9 0.0 collective-permute-done.3
  101.9 1.8 %collective-permute-start.1 = (s32[1,8]{1,0:T(1,128)S(1)}, s32[1,8]{1,0:T(1,128)S(1)}, u32[]{:S(2)}, u32[]{:S(2)}) collective-permute-start(s32[1,8]{1,0:T(1,128)S(1)} %pad_add_fusion.1), channel_id=1, source_target_pairs={{31,0},{2,1},{1,2},{4,3},{3,4},{6,5},{5,6},{8,7},{7,8},{10,9},{9,1... | collective-permute-start | bytes 104 | tf_op jit(solution)/shard_map/ppermute | solution.py:28
  103.7 0.0 collective-permute-done.2
  103.7 3.7 %collective-permute-start = (s32[1,8]{1,0:T(1,128)S(1)}, s32[1,8]{1,0:T(1,128)S(1)}, u32[]{:S(2)}, u32[]{:S(2)}) collective-permute-start(s32[1,8]{1,0:T(1,128)S(1)} %pad_add_fusion.1), channel_id=1, source_target_pairs={{1,0},{0,1},{3,2},{2,3},{5,4},{4,5},{7,6},{6,7},{9,8},{8,9},{11,10... | collective-permute-start | bytes 104 | tf_op jit(solution)/shard_map/ppermute | solution.py:28
  107.4 0.0 collective-permute-done.1
  107.4 0.8 collective-permute-done
  108.2 0.6 concatenate.23.meta_ref
  108.8 0.0 collective-permute-done.5.partner_ref.refs_3_
  108.8 6.4 %early_sums.1 = (f32[32,64,128]{2,1,0:T(8,128)}, f32[32,32,128]{2,1,0:T(8,128)}, f32[32,64,128]{2,1,0:T(8,128)}, f32[32,64,128]{2,1,0:T(8,128)}) custom-call(s32[5,9]{1,0:T(8,128)} %concatenate.23.meta_ref, f32[2,64,4096]{2,1,0:T(8,128)} %own_ref.1, f32[2,64,4096]{2,1,0:T(8,128)} %collective-permute-done.5.partner_ref.refs_3_), custom_call_target="tpu_custom_call" | custom-call | flops 8000000 | bytes 8000000 | tf_op jit(solution)/shard_map/early_sums/pallas_call | solution.py:263
  115.2 0.0 collective-permute-start.11
  115.2 0.0 collective-permute-start.6
  115.3 1.5 collective-permute-start.4
  116.7 0.8 collective-permute-done.4
  117.6 28.9 %collective-permute-done.11.refs_2_ = f32[32,64,128]{2,1,0:T(8,128)S(1)} collective-permute-done((f32[32,64,128]{2,1,0:T(8,128)}, f32[32,64,128]{2,1,0:T(8,128)S(1)}, u32[]{:S(2)}, u32[]{:S(2)}) %collective-permute-start.11) | collective-permute-done | bytes 1048608 | tf_op jit(solution)/shard_map/ppermute | solution.py:28
  146.5 0.0 collective-permute-done.8.refs_5_
  146.5 1.2 copy-done.1
  147.8 11.2 %relax_outer.1.refs_8_ = f32[2,64,4096]{2,1,0:T(8,128)} custom-call(s32[7,9]{1,0:T(8,128)S(1)} %concatenate.21.refs_0_, f32[32,64,128]{2,1,0:T(8,128)S(1)} %copy-done.1, f32[32,64,128]{2,1,0:T(8,128)S(1)} %collective-permute-done.11.refs_2_, f32[2,64,4096]{2,1,0:T(8,128)S(1)} %collective-permute-done.7.refs_3_.refs_4_, ...), custom_call_target="tpu_custom_call" | custom-call | flops 20000000 | bytes 10000000 | tf_op jit(solution)/shard_map/relax_outer/pallas_call | solution.py:282
  159.0 0.0 collective-permute-done.6.refs_2_
  159.0 0.0 collective-permute-done.10.refs_7_
  159.0 0.0 copy-done
  159.0 13.9 %relax_inner.1 = f32[2,64,4096]{2,1,0:T(8,128)} custom-call(s32[7,9]{1,0:T(8,128)S(1)} %concatenate.21.refs_0_, f32[32,64,128]{2,1,0:T(8,128)S(1)} %copy-done, f32[32,32,128]{2,1,0:T(8,128)} %collective-permute-done.6.refs_2_, f32[2,64,4096]{2,1,0:T(8,128)} %collective-permute-done.5.partner_ref.refs_3_, ...), custom_call_target="tpu_custom_call", output_to_operand_aliasing={{}: (8, {})} | custom-call | flops 20000000 | bytes 10000000 | tf_op jit(solution)/shard_map/relax_inner/pallas_call | solution.py:282
  (6 shorter events, 0.1 us)
Async XLA Ops:
  0.0 91.3 %collective-permute-start.7 = (f32[2,64,4096]{2,1,0:T(8,128)}, f32[2,64,4096]{2,1,0:T(8,128)S(1)}, u32[]{:S(2)}, u32[]{:S(2)}) collective-permute-start(f32[2,64,4096]{2,1,0:T(8,128)} %own_ref.1), channel_id=1, source_target_pairs={{31,0},{2,1},{1,2},{4,3},{3,4},{6,5},{5,6},{8,7},{7,8},{10,9},{9,1... | collective-permute-start | bytes 6291464 | tf_op jit(solution)/shard_map/ppermute | solution.py:28
  2.6 91.4 %collective-permute-start.9 = (f32[2,64,4096]{2,1,0:T(8,128)}, f32[2,64,4096]{2,1,0:T(8,128)}, u32[]{:S(2)}, u32[]{:S(2)}) collective-permute-start(f32[2,64,4096]{2,1,0:T(8,128)} %own_ref.1), channel_id=1, source_target_pairs={{30,0},{3,1},{0,2},{5,3},{2,4},{7,5},{4,6},{9,7},{6,8},{11,9},{8,1... | collective-permute-start | bytes 6291464 | tf_op jit(solution)/shard_map/ppermute | solution.py:28
  6.0 102.8 %collective-permute-start.5 = (f32[2,64,4096]{2,1,0:T(8,128)}, f32[2,64,4096]{2,1,0:T(8,128)}, u32[]{:S(2)}, u32[]{:S(2)}) collective-permute-start(f32[2,64,4096]{2,1,0:T(8,128)} %own_ref.1), channel_id=1, source_target_pairs={{1,0},{0,1},{3,2},{2,3},{5,4},{4,5},{7,6},{6,7},{9,8},{8,9},{11,10... | collective-permute-start | bytes 6291464 | tf_op jit(solution)/shard_map/ppermute | solution.py:28
  91.3 55.2 %collective-permute-start.8 = (f32[2,64,4096]{2,1,0:T(8,128)S(1)}, f32[2,64,4096]{2,1,0:T(8,128)}, u32[]{:S(2)}, u32[]{:S(2)}) collective-permute-start(f32[2,64,4096]{2,1,0:T(8,128)S(1)} %collective-permute-done.7.refs_3_.refs_4_), channel_id=1, source_target_pairs={{1,0},{0,1},{3,2},{2,3},{5,4},{4,5},{7,6},{6,7},{9,8},{8,9},{11,10... | collective-permute-start | bytes 6291464 | tf_op jit(solution)/shard_map/ppermute | solution.py:28
  94.0 65.0 %collective-permute-start.10 = (f32[2,64,4096]{2,1,0:T(8,128)}, f32[2,64,4096]{2,1,0:T(8,128)}, u32[]{:S(2)}, u32[]{:S(2)}) collective-permute-start(f32[2,64,4096]{2,1,0:T(8,128)} %collective-permute-done.9.refs_6_), channel_id=1, source_target_pairs={{1,0},{0,1},{3,2},{2,3},{5,4},{4,5},{7,6},{6,7},{9,8},{8,9},{11,10... | collective-permute-start | bytes 6291464 | tf_op jit(solution)/shard_map/ppermute | solution.py:28
  95.5 6.4 %collective-permute-start.3 = (s32[1,8]{1,0:T(1,128)S(1)}, s32[1,8]{1,0:T(1,128)S(1)}, u32[]{:S(2)}, u32[]{:S(2)}) collective-permute-start(s32[1,8]{1,0:T(1,128)S(1)} %pad_add_fusion.1), channel_id=1, source_target_pairs={{29,0},{4,1},{31,2},{6,3},{1,4},{8,5},{3,6},{10,7},{5,8},{12,9},{7... | collective-permute-start | bytes 104 | tf_op jit(solution)/shard_map/ppermute | solution.py:28
  97.2 6.5 %collective-permute-start.2 = (s32[1,8]{1,0:T(1,128)S(1)}, s32[1,8]{1,0:T(1,128)S(1)}, u32[]{:S(2)}, u32[]{:S(2)}) collective-permute-start(s32[1,8]{1,0:T(1,128)S(1)} %pad_add_fusion.1), channel_id=1, source_target_pairs={{30,0},{3,1},{0,2},{5,3},{2,4},{7,5},{4,6},{9,7},{6,8},{11,9},{8,1... | collective-permute-start | bytes 104 | tf_op jit(solution)/shard_map/ppermute | solution.py:28
  101.9 5.5 %collective-permute-start.1 = (s32[1,8]{1,0:T(1,128)S(1)}, s32[1,8]{1,0:T(1,128)S(1)}, u32[]{:S(2)}, u32[]{:S(2)}) collective-permute-start(s32[1,8]{1,0:T(1,128)S(1)} %pad_add_fusion.1), channel_id=1, source_target_pairs={{31,0},{2,1},{1,2},{4,3},{3,4},{6,5},{5,6},{8,7},{7,8},{10,9},{9,1... | collective-permute-start | bytes 104 | tf_op jit(solution)/shard_map/ppermute | solution.py:28
  103.7 4.5 %collective-permute-start = (s32[1,8]{1,0:T(1,128)S(1)}, s32[1,8]{1,0:T(1,128)S(1)}, u32[]{:S(2)}, u32[]{:S(2)}) collective-permute-start(s32[1,8]{1,0:T(1,128)S(1)} %pad_add_fusion.1), channel_id=1, source_target_pairs={{1,0},{0,1},{3,2},{2,3},{5,4},{4,5},{7,6},{6,7},{9,8},{8,9},{11,10... | collective-permute-start | bytes 104 | tf_op jit(solution)/shard_map/ppermute | solution.py:28
  115.2 31.3 %collective-permute-start.11 = (f32[32,64,128]{2,1,0:T(8,128)}, f32[32,64,128]{2,1,0:T(8,128)S(1)}, u32[]{:S(2)}, u32[]{:S(2)}) collective-permute-start(f32[32,64,128]{2,1,0:T(8,128)} %get-tuple-element.12), channel_id=1, source_target_pairs={{29,0},{4,1},{31,2},{6,3},{1,4},{8,5},{3,6},{10,7},{5,8},{12,9},{7... | collective-permute-start | bytes 3145736 | tf_op jit(solution)/shard_map/ppermute | solution.py:28
  115.2 43.7 %collective-permute-start.6 = (f32[32,32,128]{2,1,0:T(8,128)}, f32[32,32,128]{2,1,0:T(8,128)}, u32[]{:S(2)}, u32[]{:S(2)}) collective-permute-start(f32[32,32,128]{2,1,0:T(8,128)} %get-tuple-element.10), channel_id=1, source_target_pairs={{4,0},{29,1},{6,2},{31,3},{8,4},{1,5},{10,6},{3,7},{12,8},{5,9},{1... | collective-permute-start | bytes 1572872 | tf_op jit(solution)/shard_map/ppermute | solution.py:28
  115.3 2.3 %collective-permute-start.4 = (s32[2,8]{1,0:T(2,128)S(1)}, s32[2,8]{1,0:T(2,128)S(1)}, u32[]{:S(2)}, u32[]{:S(2)}) collective-permute-start(s32[2,8]{1,0:T(2,128)S(1)} %pad_add_fusion), channel_id=1, source_target_pairs={{1,0},{0,1},{3,2},{2,3},{5,4},{4,5},{7,6},{6,7},{9,8},{8,9},{11,10... | collective-permute-start | bytes 200 | tf_op jit(solution)/shard_map/ppermute | solution.py:28
  146.5 1.2 copy-start.1
  147.8 11.2 %copy-start = (f32[32,64,128]{2,1,0:T(8,128)S(1)}, f32[32,64,128]{2,1,0:T(8,128)}, u32[]{:S(2)}) copy-start(f32[32,64,128]{2,1,0:T(8,128)} %get-tuple-element.9.refs_1_) | copy-start | bytes 3145732

commit v2 on v1

--- a/solution.py
+++ b/solution.py
@@ -122,9 +122,8 @@
         lax.fori_loop(0, 2, one_box, 0)
 
 
-def relax_into(order_refs, factor_ref, out_ref, edge):
+def relax_into(order_refs, factor_ref, edge):
     chunks, rows, _ = factor_ref.shape
-    groups = rows // 8
     lane = lax.broadcasted_iota(jnp.int32, (rows, LANES), 1)
     row = lax.broadcasted_iota(jnp.int32, (8, LANES), 0)
     low_half = lane < edge
@@ -133,15 +132,14 @@
     for substep in range(SUBSTEPS):
         source = order_refs[substep % 2]
         target = order_refs[(substep + 1) % 2]
-        final = substep == SUBSTEPS - 1
-
-        def chunk(at, carry, source=source, target=target, final=final):
-            swapped_before, swapped, order = carry
+        source[0] = jnp.where(low_half, 0.0, pltpu.roll(source[chunks], edge, 1))
+        source[chunks + 1] = jnp.where(low_half, pltpu.roll(source[1], edge, 1), 0.0)
+
+        def chunk(at, carry, source=source, target=target):
+            before, order = carry
             after = source[at + 2]
-            swapped_after = pltpu.roll(after, edge, 1)
             factor = factor_ref[at]
-            beside = jnp.where(low_half, swapped, swapped_after)
-            beside += jnp.where(low_half, swapped_before, swapped)
+            beside = before + after
             beside += jnp.where(at_z_end, 0.0, pltpu.roll(order, LANES - 1, 1))
             beside += jnp.where(at_z_start, 0.0, pltpu.roll(order, 1, 1))
             upper = jnp.where(row == 7, 0.0, pltpu.roll(order[:8], 7, 0))
@@ -149,18 +147,10 @@
             beside += jnp.concatenate([order[8:], upper], axis=0)
             beside += jnp.concatenate([lower, order[: rows - 8]], axis=0)
             relaxed = order * (factor - (time_step * quartic_rate) * (order * order))
-            relaxed += (time_step * gradient_energy) * beside
-            if final:
-                for group in range(groups):
-                    picked = pl.ds(group, groups, stride=groups)
-                    out_ref.at[at][picked, :] = relaxed[group * 8 : group * 8 + 8]
-            else:
-                target[at + 1] = relaxed
-            return swapped, swapped_after, after
-
-        first = source[1]
-        zeros = jnp.zeros((rows, LANES), jnp.float32)
-        lax.fori_loop(0, chunks, chunk, (zeros, pltpu.roll(first, edge, 1), first), unroll=2)
+            target[at + 1] = relaxed + (time_step * gradient_energy) * beside
+            return order, after
+
+        lax.fori_loop(0, chunks, chunk, (source[0], source[1]), unroll=2)
 
 
 def relax_kernel(grid_tiles, target_row, source_rows, aliased, *refs):
@@ -194,9 +184,6 @@
             copy = pltpu.make_async_copy(source_refs[place].at[box], stage.at[at], sems.at[at])
             pl.when(offsets[0])(copy.start)
             work.append((at, offsets, copy))
-    for order_ref in (order_a, order_b):
-        order_ref[0] = jnp.zeros((rows, LANES), jnp.float32)
-        order_ref[chunks + 1] = jnp.zeros((rows, LANES), jnp.float32)
     if target_row == 2:
         total_ref[...] = total_in_ref[...] + part_ref[...]
     else:
@@ -209,27 +196,50 @@
     base = 1.0 + time_step * (growth_rate - 6.0 * gradient_energy)
     factor_ref = result_ref
 
+    low_half = lax.broadcasted_iota(jnp.int32, (8, LANES), 1) < rows
+    pairs = chunks // 2
+
+    def interleave(first, second):
+        even = jnp.where(low_half, first, pltpu.roll(second, rows, 1))
+        odd = jnp.where(low_half, pltpu.roll(first, rows, 1), second)
+        return even, odd
+
     def prepare(at, carry):
         for group in range(groups):
             picked = pl.ds(group, groups, stride=groups)
             into = pl.ds(group * 8, 8)
-            order_a[at + 1, into, :] = target_stage.at[at][picked, :]
-            factor_ref[at, into, :] = (
-                base - (time_step * 2.0 * coupling) * total_ref.at[at][picked, :]
+            even, odd = interleave(
+                target_stage.at[at][picked, :], target_stage.at[at + pairs][picked, :]
             )
+            order_a[2 * at + 1, into, :] = even
+            order_a[2 * at + 2, into, :] = odd
+            even, odd = interleave(total_ref.at[at][picked, :], total_ref.at[at + pairs][picked, :])
+            factor_ref[2 * at, into, :] = base - (time_step * 2.0 * coupling) * even
+            factor_ref[2 * at + 1, into, :] = base - (time_step * 2.0 * coupling) * odd
         return carry
 
-    lax.fori_loop(0, chunks, prepare, 0, unroll=2)
-    relax_into((order_a, order_b), factor_ref, total_ref, rows)
+    lax.fori_loop(0, pairs, prepare, 0)
+    orders = (order_a, order_b)
+    relax_into(orders, factor_ref, rows)
+    relaxed_ref = orders[SUBSTEPS % 2]
 
     def deliver(at, carry):
-        columns = pl.ds(pl.multiple_of(at * LANES, LANES), LANES)
-        pltpu.make_async_copy(
-            total_ref.at[at], out_ref.at[out_slot, :, columns], sems.at[2 * count]
-        ).start()
+        for group in range(groups):
+            picked = pl.ds(group, groups, stride=groups)
+            even = relaxed_ref[2 * at + 1, group * 8 : group * 8 + 8, :]
+            odd = relaxed_ref[2 * at + 2, group * 8 : group * 8 + 8, :]
+            total_ref.at[at][picked, :] = jnp.where(low_half, even, pltpu.roll(odd, rows, 1))
+            total_ref.at[at + pairs][picked, :] = jnp.where(
+                low_half, pltpu.roll(even, rows, 1), odd
+            )
+        for chunk in (at, at + pairs):
+            columns = pl.ds(pl.multiple_of(chunk * LANES, LANES), LANES)
+            pltpu.make_async_copy(
+                total_ref.at[chunk], out_ref.at[out_slot, :, columns], sems.at[2 * count]
+            ).start()
         return carry
 
-    lax.fori_loop(0, chunks, deliver, 0)
+    lax.fori_loop(0, pairs, deliver, 0)
     pltpu.make_async_copy(total_ref, total_ref, sems.at[2 * count]).wait()
 
 

time: 173 us -> 175 us (1.012)
    pallas_call x2, Pallas kernels: 25.2 us -> 26.9 us  [relax(): pl.pallas_call(functools.partial(relax_kernel, devices, target_row, sourc...]
  transfers between devices with their start and end apart: 12 -> 12, of which waited for: 5 -> 5; matrix products, arithmetic and copies ran while one was open for 1% -> 1% of each run, Pallas kernels for 10% -> 11%
where the time goes in v2:
time: 175 us
  waiting for transfers between devices  118 us (67%)
  Pallas kernels  33.3 us (19%)
  starting transfers between devices  19.8 us (11%)
  local copies, waits for them, and re-layouts  2.64 us (2%)
    ppermute x12, waiting for transfers between devices, from_outward(): return lax.ppermute(value, 'dev', pairs)  118 us
    pallas_call x2, Pallas kernels, relax(): pl.pallas_call(functools.partial(relax_kernel, devices, target_row, sourc...  26.9 us
    ppermute x12, starting transfers between devices, from_outward(): return lax.ppermute(value, 'dev', pairs)  19.8 us
    pallas_call x1, Pallas kernels, on_device(): pl.pallas_call(functools.partial(early_kernel, devices), out_shape=(box_s...  6.41 us
  transfers between devices with their start and end apart: 12, of which 5 were waited for; matrix products, arithmetic and copies ran while one was open for 1% of the time, Pallas kernels for 11%

profile of v2, /device:TPU:1, one launch (start us, length us, event | category | flops | bytes accessed | tf_op | source)
XLA Modules:
  0.0 174.7 jit_solution(3589791066951615825)
XLA Ops:
  0.0 2.6 %collective-permute-start.7 = (f32[2,64,4096]{2,1,0:T(8,128)}, f32[2,64,4096]{2,1,0:T(8,128)S(1)}, u32[]{:S(2)}, u32[]{:S(2)}) collective-permute-start(f32[2,64,4096]{2,1,0:T(8,128)} %own_ref.1), channel_id=1, source_target_pairs={{31,0},{2,1},{1,2},{4,3},{3,4},{6,5},{5,6},{8,7},{7,8},{10,9},{9,1... | collective-permute-start | bytes 6291464 | tf_op jit(solution)/shard_map/ppermute | solution.py:28
  2.6 3.4 %collective-permute-start.9 = (f32[2,64,4096]{2,1,0:T(8,128)}, f32[2,64,4096]{2,1,0:T(8,128)}, u32[]{:S(2)}, u32[]{:S(2)}) collective-permute-start(f32[2,64,4096]{2,1,0:T(8,128)} %own_ref.1), channel_id=1, source_target_pairs={{30,0},{3,1},{0,2},{5,3},{2,4},{7,5},{4,6},{9,7},{6,8},{11,9},{8,1... | collective-permute-start | bytes 6291464 | tf_op jit(solution)/shard_map/ppermute | solution.py:28
  6.0 0.4 collective-permute-start.5
  6.4 84.9 %collective-permute-done.7.refs_3_.refs_4_ = f32[2,64,4096]{2,1,0:T(8,128)S(1)} collective-permute-done((f32[2,64,4096]{2,1,0:T(8,128)}, f32[2,64,4096]{2,1,0:T(8,128)S(1)}, u32[]{:S(2)}, u32[]{:S(2)}) %collective-permute-start.7) | collective-permute-done | bytes 2097184 | tf_op jit(solution)/shard_map/ppermute | solution.py:28
  91.3 0.0 collective-permute-start.8
  91.3 2.7 %collective-permute-done.9.refs_6_ = f32[2,64,4096]{2,1,0:T(8,128)} collective-permute-done((f32[2,64,4096]{2,1,0:T(8,128)}, f32[2,64,4096]{2,1,0:T(8,128)}, u32[]{:S(2)}, u32[]{:S(2)}) %collective-permute-start.9) | collective-permute-done | bytes 2097184 | tf_op jit(solution)/shard_map/ppermute | solution.py:28
  94.0 0.0 collective-permute-start.10
  94.0 0.8 reshape.10
  94.8 0.7 pad_add_fusion.1
  95.5 1.6 collective-permute-start.3
  97.2 4.7 %collective-permute-start.2 = (s32[1,8]{1,0:T(1,128)S(1)}, s32[1,8]{1,0:T(1,128)S(1)}, u32[]{:S(2)}, u32[]{:S(2)}) collective-permute-start(s32[1,8]{1,0:T(1,128)S(1)} %pad_add_fusion.1), channel_id=1, source_target_pairs={{30,0},{3,1},{0,2},{5,3},{2,4},{7,5},{4,6},{9,7},{6,8},{11,9},{8,1... | collective-permute-start | bytes 104 | tf_op jit(solution)/shard_map/ppermute | solution.py:28
  101.9 0.0 collective-permute-done.3
  101.9 1.8 %collective-permute-start.1 = (s32[1,8]{1,0:T(1,128)S(1)}, s32[1,8]{1,0:T(1,128)S(1)}, u32[]{:S(2)}, u32[]{:S(2)}) collective-permute-start(s32[1,8]{1,0:T(1,128)S(1)} %pad_add_fusion.1), channel_id=1, source_target_pairs={{31,0},{2,1},{1,2},{4,3},{3,4},{6,5},{5,6},{8,7},{7,8},{10,9},{9,1... | collective-permute-start | bytes 104 | tf_op jit(solution)/shard_map/ppermute | solution.py:28
  103.7 0.0 collective-permute-done.2
  103.7 3.7 %collective-permute-start = (s32[1,8]{1,0:T(1,128)S(1)}, s32[1,8]{1,0:T(1,128)S(1)}, u32[]{:S(2)}, u32[]{:S(2)}) collective-permute-start(s32[1,8]{1,0:T(1,128)S(1)} %pad_add_fusion.1), channel_id=1, source_target_pairs={{1,0},{0,1},{3,2},{2,3},{5,4},{4,5},{7,6},{6,7},{9,8},{8,9},{11,10... | collective-permute-start | bytes 104 | tf_op jit(solution)/shard_map/ppermute | solution.py:28
  107.4 0.0 collective-permute-done.1
  107.4 0.8 collective-permute-done
  108.2 0.6 concatenate.23.meta_ref
  108.8 0.0 collective-permute-done.5.partner_ref.refs_3_
  108.8 6.4 %early_sums.1 = (f32[32,64,128]{2,1,0:T(8,128)}, f32[32,32,128]{2,1,0:T(8,128)}, f32[32,64,128]{2,1,0:T(8,128)}, f32[32,64,128]{2,1,0:T(8,128)}) custom-call(s32[5,9]{1,0:T(8,128)} %concatenate.23.meta_ref, f32[2,64,4096]{2,1,0:T(8,128)} %own_ref.1, f32[2,64,4096]{2,1,0:T(8,128)} %collective-permute-done.5.partner_ref.refs_3_), custom_call_target="tpu_custom_call" | custom-call | flops 8000000 | bytes 8000000 | tf_op jit(solution)/shard_map/early_sums/pallas_call | solution.py:273
  115.2 0.0 collective-permute-start.11
  115.2 0.0 collective-permute-start.6
  115.3 1.5 collective-permute-start.4
  116.7 0.8 collective-permute-done.4
  117.6 28.9 %collective-permute-done.11.refs_2_ = f32[32,64,128]{2,1,0:T(8,128)S(1)} collective-permute-done((f32[32,64,128]{2,1,0:T(8,128)}, f32[32,64,128]{2,1,0:T(8,128)S(1)}, u32[]{:S(2)}, u32[]{:S(2)}) %collective-permute-start.11) | collective-permute-done | bytes 1048608 | tf_op jit(solution)/shard_map/ppermute | solution.py:28
  146.5 0.0 collective-permute-done.8.refs_5_
  146.5 1.2 copy-done.1
  147.8 12.1 %relax_outer.1.refs_8_ = f32[2,64,4096]{2,1,0:T(8,128)} custom-call(s32[7,9]{1,0:T(8,128)S(1)} %concatenate.21.refs_0_, f32[32,64,128]{2,1,0:T(8,128)S(1)} %copy-done.1, f32[32,64,128]{2,1,0:T(8,128)S(1)} %collective-permute-done.11.refs_2_, f32[2,64,4096]{2,1,0:T(8,128)S(1)} %collective-permute-done.7.refs_3_.refs_4_, ...), custom_call_target="tpu_custom_call" | custom-call | flops 20000000 | bytes 10000000 | tf_op jit(solution)/shard_map/relax_outer/pallas_call | solution.py:292
  159.9 0.0 collective-permute-done.6.refs_2_
  159.9 0.0 collective-permute-done.10.refs_7_
  159.9 0.0 copy-done
  159.9 14.8 %relax_inner.1 = f32[2,64,4096]{2,1,0:T(8,128)} custom-call(s32[7,9]{1,0:T(8,128)S(1)} %concatenate.21.refs_0_, f32[32,64,128]{2,1,0:T(8,128)S(1)} %copy-done, f32[32,32,128]{2,1,0:T(8,128)} %collective-permute-done.6.refs_2_, f32[2,64,4096]{2,1,0:T(8,128)} %collective-permute-done.5.partner_ref.refs_3_, ...), custom_call_target="tpu_custom_call", output_to_operand_aliasing={{}: (8, {})} | custom-call | flops 20000000 | bytes 10000000 | tf_op jit(solution)/shard_map/relax_inner/pallas_call | solution.py:292
  (6 shorter events, 0.1 us)
Async XLA Ops:
  0.0 91.3 %collective-permute-start.7 = (f32[2,64,4096]{2,1,0:T(8,128)}, f32[2,64,4096]{2,1,0:T(8,128)S(1)}, u32[]{:S(2)}, u32[]{:S(2)}) collective-permute-start(f32[2,64,4096]{2,1,0:T(8,128)} %own_ref.1), channel_id=1, source_target_pairs={{31,0},{2,1},{1,2},{4,3},{3,4},{6,5},{5,6},{8,7},{7,8},{10,9},{9,1... | collective-permute-start | bytes 6291464 | tf_op jit(solution)/shard_map/ppermute | solution.py:28
  2.6 91.4 %collective-permute-start.9 = (f32[2,64,4096]{2,1,0:T(8,128)}, f32[2,64,4096]{2,1,0:T(8,128)}, u32[]{:S(2)}, u32[]{:S(2)}) collective-permute-start(f32[2,64,4096]{2,1,0:T(8,128)} %own_ref.1), channel_id=1, source_target_pairs={{30,0},{3,1},{0,2},{5,3},{2,4},{7,5},{4,6},{9,7},{6,8},{11,9},{8,1... | collective-permute-start | bytes 6291464 | tf_op jit(solution)/shard_map/ppermute | solution.py:28
  6.0 102.8 %collective-permute-start.5 = (f32[2,64,4096]{2,1,0:T(8,128)}, f32[2,64,4096]{2,1,0:T(8,128)}, u32[]{:S(2)}, u32[]{:S(2)}) collective-permute-start(f32[2,64,4096]{2,1,0:T(8,128)} %own_ref.1), channel_id=1, source_target_pairs={{1,0},{0,1},{3,2},{2,3},{5,4},{4,5},{7,6},{6,7},{9,8},{8,9},{11,10... | collective-permute-start | bytes 6291464 | tf_op jit(solution)/shard_map/ppermute | solution.py:28
  91.3 55.2 %collective-permute-start.8 = (f32[2,64,4096]{2,1,0:T(8,128)S(1)}, f32[2,64,4096]{2,1,0:T(8,128)}, u32[]{:S(2)}, u32[]{:S(2)}) collective-permute-start(f32[2,64,4096]{2,1,0:T(8,128)S(1)} %collective-permute-done.7.refs_3_.refs_4_), channel_id=1, source_target_pairs={{1,0},{0,1},{3,2},{2,3},{5,4},{4,5},{7,6},{6,7},{9,8},{8,9},{11,10... | collective-permute-start | bytes 6291464 | tf_op jit(solution)/shard_map/ppermute | solution.py:28
  94.0 65.8 %collective-permute-start.10 = (f32[2,64,4096]{2,1,0:T(8,128)}, f32[2,64,4096]{2,1,0:T(8,128)}, u32[]{:S(2)}, u32[]{:S(2)}) collective-permute-start(f32[2,64,4096]{2,1,0:T(8,128)} %collective-permute-done.9.refs_6_), channel_id=1, source_target_pairs={{1,0},{0,1},{3,2},{2,3},{5,4},{4,5},{7,6},{6,7},{9,8},{8,9},{11,10... | collective-permute-start | bytes 6291464 | tf_op jit(solution)/shard_map/ppermute | solution.py:28
  95.5 6.4 %collective-permute-start.3 = (s32[1,8]{1,0:T(1,128)S(1)}, s32[1,8]{1,0:T(1,128)S(1)}, u32[]{:S(2)}, u32[]{:S(2)}) collective-permute-start(s32[1,8]{1,0:T(1,128)S(1)} %pad_add_fusion.1), channel_id=1, source_target_pairs={{29,0},{4,1},{31,2},{6,3},{1,4},{8,5},{3,6},{10,7},{5,8},{12,9},{7... | collective-permute-start | bytes 104 | tf_op jit(solution)/shard_map/ppermute | solution.py:28
  97.2 6.5 %collective-permute-start.2 = (s32[1,8]{1,0:T(1,128)S(1)}, s32[1,8]{1,0:T(1,128)S(1)}, u32[]{:S(2)}, u32[]{:S(2)}) collective-permute-start(s32[1,8]{1,0:T(1,128)S(1)} %pad_add_fusion.1), channel_id=1, source_target_pairs={{30,0},{3,1},{0,2},{5,3},{2,4},{7,5},{4,6},{9,7},{6,8},{11,9},{8,1... | collective-permute-start | bytes 104 | tf_op jit(solution)/shard_map/ppermute | solution.py:28
  101.9 5.5 %collective-permute-start.1 = (s32[1,8]{1,0:T(1,128)S(1)}, s32[1,8]{1,0:T(1,128)S(1)}, u32[]{:S(2)}, u32[]{:S(2)}) collective-permute-start(s32[1,8]{1,0:T(1,128)S(1)} %pad_add_fusion.1), channel_id=1, source_target_pairs={{31,0},{2,1},{1,2},{4,3},{3,4},{6,5},{5,6},{8,7},{7,8},{10,9},{9,1... | collective-permute-start | bytes 104 | tf_op jit(solution)/shard_map/ppermute | solution.py:28
  103.7 4.5 %collective-permute-start = (s32[1,8]{1,0:T(1,128)S(1)}, s32[1,8]{1,0:T(1,128)S(1)}, u32[]{:S(2)}, u32[]{:S(2)}) collective-permute-start(s32[1,8]{1,0:T(1,128)S(1)} %pad_add_fusion.1), channel_id=1, source_target_pairs={{1,0},{0,1},{3,2},{2,3},{5,4},{4,5},{7,6},{6,7},{9,8},{8,9},{11,10... | collective-permute-start | bytes 104 | tf_op jit(solution)/shard_map/ppermute | solution.py:28
  115.2 31.3 %collective-permute-start.11 = (f32[32,64,128]{2,1,0:T(8,128)}, f32[32,64,128]{2,1,0:T(8,128)S(1)}, u32[]{:S(2)}, u32[]{:S(2)}) collective-permute-start(f32[32,64,128]{2,1,0:T(8,128)} %get-tuple-element.12), channel_id=1, source_target_pairs={{29,0},{4,1},{31,2},{6,3},{1,4},{8,5},{3,6},{10,7},{5,8},{12,9},{7... | collective-permute-start | bytes 3145736 | tf_op jit(solution)/shard_map/ppermute | solution.py:28
  115.2 44.6 %collective-permute-start.6 = (f32[32,32,128]{2,1,0:T(8,128)}, f32[32,32,128]{2,1,0:T(8,128)}, u32[]{:S(2)}, u32[]{:S(2)}) collective-permute-start(f32[32,32,128]{2,1,0:T(8,128)} %get-tuple-element.10), channel_id=1, source_target_pairs={{4,0},{29,1},{6,2},{31,3},{8,4},{1,5},{10,6},{3,7},{12,8},{5,9},{1... | collective-permute-start | bytes 1572872 | tf_op jit(solution)/shard_map/ppermute | solution.py:28
  115.3 2.3 %collective-permute-start.4 = (s32[2,8]{1,0:T(2,128)S(1)}, s32[2,8]{1,0:T(2,128)S(1)}, u32[]{:S(2)}, u32[]{:S(2)}) collective-permute-start(s32[2,8]{1,0:T(2,128)S(1)} %pad_add_fusion), channel_id=1, source_target_pairs={{1,0},{0,1},{3,2},{2,3},{5,4},{4,5},{7,6},{6,7},{9,8},{8,9},{11,10... | collective-permute-start | bytes 200 | tf_op jit(solution)/shard_map/ppermute | solution.py:28
  146.5 1.2 copy-start.1
  147.8 12.1 %copy-start = (f32[32,64,128]{2,1,0:T(8,128)S(1)}, f32[32,64,128]{2,1,0:T(8,128)}, u32[]{:S(2)}) copy-start(f32[32,64,128]{2,1,0:T(8,128)} %get-tuple-element.9.refs_1_) | copy-start | bytes 3145732

commit v3 on v1

--- a/solution.py
+++ b/solution.py
@@ -122,7 +122,7 @@
         lax.fori_loop(0, 2, one_box, 0)
 
 
-def relax_into(order_refs, factor_ref, out_ref, edge):
+def relax_into(order_refs, factor_ref, out_ref, edge, deliver):
     chunks, rows, _ = factor_ref.shape
     groups = rows // 8
     lane = lax.broadcasted_iota(jnp.int32, (rows, LANES), 1)
@@ -154,6 +154,7 @@
                 for group in range(groups):
                     picked = pl.ds(group, groups, stride=groups)
                     out_ref.at[at][picked, :] = relaxed[group * 8 : group * 8 + 8]
+                deliver(at)
             else:
                 target[at + 1] = relaxed
             return swapped, swapped_after, after
@@ -167,7 +168,7 @@
     meta_ref, total_in_ref, part_ref, target_ref = refs[:4]
     count = len(source_rows)
     source_refs = refs[4 : 4 + count]
-    out_ref, order_a, order_b, total_ref, result_ref, stage, target_stage, sems = refs[
+    out_ref, order_a, order_b, total_ref, result_ref, stage, target_stage, part_stage, sems = refs[
         4 + count + aliased :
     ]
     chunks, rows, _ = total_ref.shape
@@ -175,6 +176,11 @@
     groups = rows // 8
     slot, out_slot = target_slots(meta_ref, target_row)
     target = box_anchor(meta_ref, target_row, slot)
+
+    total_copy = pltpu.make_async_copy(total_in_ref, total_ref, sems.at[2 * count + 1])
+    total_copy.start()
+    part_copy = pltpu.make_async_copy(part_ref, part_stage, sems.at[2 * count + 2])
+    part_copy.start()
 
     def fetch(at, carry):
         columns = pl.ds(pl.multiple_of(at * LANES, LANES), LANES)
@@ -197,12 +203,13 @@
     for order_ref in (order_a, order_b):
         order_ref[0] = jnp.zeros((rows, LANES), jnp.float32)
         order_ref[chunks + 1] = jnp.zeros((rows, LANES), jnp.float32)
+    total_copy.wait()
+    part_copy.wait()
     if target_row == 2:
-        total_ref[...] = total_in_ref[...] + part_ref[...]
+        total_ref[...] += part_stage[...]
     else:
-        total_ref[...] = total_in_ref[...]
         near_row = pl.multiple_of((1 - meta_ref[0, 8]) * half, half)
-        total_ref[:, pl.ds(near_row, half), :] += part_ref[...]
+        total_ref[:, pl.ds(near_row, half), :] += part_stage[...]
     for at, offsets, copy in work:
         add_squares(total_ref, stage.at[at], offsets, ready=copy.wait)
     pltpu.make_async_copy(target_stage, target_stage, sems.at[2 * count]).wait()
@@ -220,16 +227,14 @@
         return carry
 
     lax.fori_loop(0, chunks, prepare, 0, unroll=2)
-    relax_into((order_a, order_b), factor_ref, total_ref, rows)
-
-    def deliver(at, carry):
+
+    def deliver(at):
         columns = pl.ds(pl.multiple_of(at * LANES, LANES), LANES)
         pltpu.make_async_copy(
             total_ref.at[at], out_ref.at[out_slot, :, columns], sems.at[2 * count]
         ).start()
-        return carry
-
-    lax.fori_loop(0, chunks, deliver, 0)
+
+    relax_into((order_a, order_b), factor_ref, total_ref, rows, deliver)
     pltpu.make_async_copy(total_ref, total_ref, sems.at[2 * count]).wait()
 
 
@@ -282,7 +287,7 @@
         return pl.pallas_call(
             functools.partial(relax_kernel, devices, target_row, source_rows, aliased),
             out_shape=jax.ShapeDtypeStruct(grain_boxes.shape, jnp.float32),
-            in_specs=[smem, vmem, vmem] + [anywhere] * (1 + count + aliased),
+            in_specs=[smem] + [anywhere] * (3 + count + aliased),
             out_specs=anywhere,
             input_output_aliases={4 + count: 0} if aliased else {},
             scratch_shapes=[
@@ -292,10 +297,11 @@
                 box_scratch,
                 pltpu.VMEM((2 * count, box_edge, area), jnp.float32),
                 box_scratch,
-                pltpu.SemaphoreType.DMA((2 * count + 1,)),
+                pltpu.VMEM(part.shape, jnp.float32),
+                pltpu.SemaphoreType.DMA((2 * count + 3,)),
             ],
             name="relax_outer" if target_row == 2 else "relax_inner",
-            compiler_params=pltpu.CompilerParams(vmem_limit_bytes=32 * 1024 * 1024),
+            compiler_params=pltpu.CompilerParams(vmem_limit_bytes=60 * 1024 * 1024),
             cost_estimate=pl.CostEstimate(
                 flops=20_000_000, bytes_accessed=10_000_000, transcendentals=0
             ),

time: 173 us -> 174 us (level)
  transfers between devices with their start and end apart: 12 -> 12, of which waited for: 5 -> 5; matrix products, arithmetic and copies ran while one was open for 1% -> 2% of each run, Pallas kernels for 10% -> 11%
where the time goes in v3:
time: 174 us; the launch traced here: 173 us
  waiting for transfers between devices  118 us (68%)
  Pallas kernels  32.3 us (19%)
  starting transfers between devices  19.8 us (11%)
  local copies, waits for them, and re-layouts  3.04 us (2%)
    ppermute x12, waiting for transfers between devices, from_outward(): return lax.ppermute(value, 'dev', pairs)  118 us
    pallas_call x2, Pallas kernels, relax(): pl.pallas_call(functools.partial(relax_kernel, devices, target_row, sourc...  25.8 us
    ppermute x12, starting transfers between devices, from_outward(): return lax.ppermute(value, 'dev', pairs)  19.8 us
    pallas_call x1, Pallas kernels, on_device(): pl.pallas_call(functools.partial(early_kernel, devices), out_shape=(box_s...  6.44 us
  transfers between devices with their start and end apart: 12, of which 5 were waited for; matrix products, arithmetic and copies ran while one was open for 2% of the time, Pallas kernels for 11%

profile of v3, /device:TPU:1, one launch (start us, length us, event | category | flops | bytes accessed | tf_op | source)
XLA Modules:
  0.0 173.5 jit_solution(16365590630766159925)
XLA Ops:
  0.0 2.6 %collective-permute-start.7 = (f32[2,64,4096]{2,1,0:T(8,128)}, f32[2,64,4096]{2,1,0:T(8,128)S(1)}, u32[]{:S(2)}, u32[]{:S(2)}) collective-permute-start(f32[2,64,4096]{2,1,0:T(8,128)} %own_ref.1), channel_id=1, source_target_pairs={{31,0},{2,1},{1,2},{4,3},{3,4},{6,5},{5,6},{8,7},{7,8},{10,9},{9,1... | collective-permute-start | bytes 6291464 | tf_op jit(solution)/shard_map/ppermute | solution.py:28
  2.6 3.4 %collective-permute-start.9 = (f32[2,64,4096]{2,1,0:T(8,128)}, f32[2,64,4096]{2,1,0:T(8,128)}, u32[]{:S(2)}, u32[]{:S(2)}) collective-permute-start(f32[2,64,4096]{2,1,0:T(8,128)} %own_ref.1), channel_id=1, source_target_pairs={{30,0},{3,1},{0,2},{5,3},{2,4},{7,5},{4,6},{9,7},{6,8},{11,9},{8,1... | collective-permute-start | bytes 6291464 | tf_op jit(solution)/shard_map/ppermute | solution.py:28
  6.0 0.4 collective-permute-start.5
  6.4 84.9 %collective-permute-done.7.refs_3_.refs_4_ = f32[2,64,4096]{2,1,0:T(8,128)S(1)} collective-permute-done((f32[2,64,4096]{2,1,0:T(8,128)}, f32[2,64,4096]{2,1,0:T(8,128)S(1)}, u32[]{:S(2)}, u32[]{:S(2)}) %collective-permute-start.7) | collective-permute-done | bytes 2097184 | tf_op jit(solution)/shard_map/ppermute | solution.py:28
  91.3 0.0 collective-permute-start.8
  91.3 2.7 %collective-permute-done.9.refs_6_ = f32[2,64,4096]{2,1,0:T(8,128)} collective-permute-done((f32[2,64,4096]{2,1,0:T(8,128)}, f32[2,64,4096]{2,1,0:T(8,128)}, u32[]{:S(2)}, u32[]{:S(2)}) %collective-permute-start.9) | collective-permute-done | bytes 2097184 | tf_op jit(solution)/shard_map/ppermute | solution.py:28
  94.0 0.0 collective-permute-start.10
  94.0 0.8 reshape.10
  94.8 0.7 pad_add_fusion.1
  95.5 1.6 collective-permute-start.3
  97.2 4.7 %collective-permute-start.2 = (s32[1,8]{1,0:T(1,128)S(1)}, s32[1,8]{1,0:T(1,128)S(1)}, u32[]{:S(2)}, u32[]{:S(2)}) collective-permute-start(s32[1,8]{1,0:T(1,128)S(1)} %pad_add_fusion.1), channel_id=1, source_target_pairs={{30,0},{3,1},{0,2},{5,3},{2,4},{7,5},{4,6},{9,7},{6,8},{11,9},{8,1... | collective-permute-start | bytes 104 | tf_op jit(solution)/shard_map/ppermute | solution.py:28
  101.9 0.0 collective-permute-done.3
  101.9 1.8 %collective-permute-start.1 = (s32[1,8]{1,0:T(1,128)S(1)}, s32[1,8]{1,0:T(1,128)S(1)}, u32[]{:S(2)}, u32[]{:S(2)}) collective-permute-start(s32[1,8]{1,0:T(1,128)S(1)} %pad_add_fusion.1), channel_id=1, source_target_pairs={{31,0},{2,1},{1,2},{4,3},{3,4},{6,5},{5,6},{8,7},{7,8},{10,9},{9,1... | collective-permute-start | bytes 104 | tf_op jit(solution)/shard_map/ppermute | solution.py:28
  103.7 0.0 collective-permute-done.2
  103.7 3.7 %collective-permute-start = (s32[1,8]{1,0:T(1,128)S(1)}, s32[1,8]{1,0:T(1,128)S(1)}, u32[]{:S(2)}, u32[]{:S(2)}) collective-permute-start(s32[1,8]{1,0:T(1,128)S(1)} %pad_add_fusion.1), channel_id=1, source_target_pairs={{1,0},{0,1},{3,2},{2,3},{5,4},{4,5},{7,6},{6,7},{9,8},{8,9},{11,10... | collective-permute-start | bytes 104 | tf_op jit(solution)/shard_map/ppermute | solution.py:28
  107.4 0.0 collective-permute-done.1
  107.4 0.8 collective-permute-done
  108.2 0.6 concatenate.23.meta_ref
  108.8 0.0 collective-permute-done.5.partner_ref.refs_3_
  108.8 6.4 %early_sums.1 = (f32[32,64,128]{2,1,0:T(8,128)}, f32[32,32,128]{2,1,0:T(8,128)}, f32[32,64,128]{2,1,0:T(8,128)}, f32[32,64,128]{2,1,0:T(8,128)}) custom-call(s32[5,9]{1,0:T(8,128)} %concatenate.23.meta_ref, f32[2,64,4096]{2,1,0:T(8,128)} %own_ref.1, f32[2,64,4096]{2,1,0:T(8,128)} %collective-permute-done.5.partner_ref.refs_3_), custom_call_target="tpu_custom_call" | custom-call | flops 8000000 | bytes 8000000 | tf_op jit(solution)/shard_map/early_sums/pallas_call | solution.py:268
  115.3 0.0 collective-permute-start.11
  115.3 0.1 collective-permute-start.6
  115.4 1.4 collective-permute-start.4
  116.8 0.8 collective-permute-done.4
  117.6 0.6 concatenate.21.refs_0_
  118.2 28.3 %collective-permute-done.11.refs_2_ = f32[32,64,128]{2,1,0:T(8,128)S(1)} collective-permute-done((f32[32,64,128]{2,1,0:T(8,128)}, f32[32,64,128]{2,1,0:T(8,128)S(1)}, u32[]{:S(2)}, u32[]{:S(2)}) %collective-permute-start.11) | collective-permute-done | bytes 1048608 | tf_op jit(solution)/shard_map/ppermute | solution.py:28
  146.6 0.0 collective-permute-done.8.refs_5_
  146.6 1.0 copy-done.1
  147.6 12.2 %relax_outer.1.refs_8_ = f32[2,64,4096]{2,1,0:T(8,128)} custom-call(s32[7,9]{1,0:T(8,128)} %concatenate.21.refs_0_, f32[32,64,128]{2,1,0:T(8,128)} %get-tuple-element.11.refs_1_, f32[32,64,128]{2,1,0:T(8,128)} %copy-done.1, f32[2,64,4096]{2,1,0:T(8,128)} %copy-done, f32[2,64,4096]{2,1,0:T(8,128)} %copy-done, f32[2,64,4096]{2,1,0:T(8,128)} %collective-permute-done.8.refs_5_, ...), custom_call_target="tpu_custom_call" | custom-call | flops 20000000 | bytes 10000000 | tf_op jit(solution)/shard_map/relax_outer/pallas_call | solution.py:287
  159.8 0.0 collective-permute-done.6.refs_2_
  159.8 0.0 collective-permute-done.10.refs_7_
  159.8 13.7 %relax_inner.1 = f32[2,64,4096]{2,1,0:T(8,128)} custom-call(s32[7,9]{1,0:T(8,128)} %concatenate.21.refs_0_, f32[32,64,128]{2,1,0:T(8,128)} %get-tuple-element.9.refs_1_, f32[32,32,128]{2,1,0:T(8,128)} %collective-permute-done.6.refs_2_, f32[2,64,4096]{2,1,0:T(8,128)} %collective-permute-done.5.partner_ref.refs_3_, ...), custom_call_target="tpu_custom_call", output_to_operand_aliasing={{}: (8, {})} | custom-call | flops 20000000 | bytes 10000000 | tf_op jit(solution)/shard_map/relax_inner/pallas_call | solution.py:287
  (6 shorter events, 0.1 us)
Async XLA Ops:
  0.0 91.3 %collective-permute-start.7 = (f32[2,64,4096]{2,1,0:T(8,128)}, f32[2,64,4096]{2,1,0:T(8,128)S(1)}, u32[]{:S(2)}, u32[]{:S(2)}) collective-permute-start(f32[2,64,4096]{2,1,0:T(8,128)} %own_ref.1), channel_id=1, source_target_pairs={{31,0},{2,1},{1,2},{4,3},{3,4},{6,5},{5,6},{8,7},{7,8},{10,9},{9,1... | collective-permute-start | bytes 6291464 | tf_op jit(solution)/shard_map/ppermute | solution.py:28
  2.6 91.4 %collective-permute-start.9 = (f32[2,64,4096]{2,1,0:T(8,128)}, f32[2,64,4096]{2,1,0:T(8,128)}, u32[]{:S(2)}, u32[]{:S(2)}) collective-permute-start(f32[2,64,4096]{2,1,0:T(8,128)} %own_ref.1), channel_id=1, source_target_pairs={{30,0},{3,1},{0,2},{5,3},{2,4},{7,5},{4,6},{9,7},{6,8},{11,9},{8,1... | collective-permute-start | bytes 6291464 | tf_op jit(solution)/shard_map/ppermute | solution.py:28
  6.0 102.8 %collective-permute-start.5 = (f32[2,64,4096]{2,1,0:T(8,128)}, f32[2,64,4096]{2,1,0:T(8,128)}, u32[]{:S(2)}, u32[]{:S(2)}) collective-permute-start(f32[2,64,4096]{2,1,0:T(8,128)} %own_ref.1), channel_id=1, source_target_pairs={{1,0},{0,1},{3,2},{2,3},{5,4},{4,5},{7,6},{6,7},{9,8},{8,9},{11,10... | collective-permute-start | bytes 6291464 | tf_op jit(solution)/shard_map/ppermute | solution.py:28
  91.3 23.9 %copy-start = (f32[2,64,4096]{2,1,0:T(8,128)}, f32[2,64,4096]{2,1,0:T(8,128)S(1)}, u32[]{:S(2)}) copy-start(f32[2,64,4096]{2,1,0:T(8,128)S(1)} %collective-permute-done.7.refs_3_.refs_4_) | copy-start | bytes 6291460
  91.3 55.2 %collective-permute-start.8 = (f32[2,64,4096]{2,1,0:T(8,128)S(1)}, f32[2,64,4096]{2,1,0:T(8,128)}, u32[]{:S(2)}, u32[]{:S(2)}) collective-permute-start(f32[2,64,4096]{2,1,0:T(8,128)S(1)} %collective-permute-done.7.refs_3_.refs_4_), channel_id=1, source_target_pairs={{1,0},{0,1},{3,2},{2,3},{5,4},{4,5},{7,6},{6,7},{9,8},{8,9},{11,10... | collective-permute-start | bytes 6291464 | tf_op jit(solution)/shard_map/ppermute | solution.py:28
  94.0 65.8 %collective-permute-start.10 = (f32[2,64,4096]{2,1,0:T(8,128)}, f32[2,64,4096]{2,1,0:T(8,128)}, u32[]{:S(2)}, u32[]{:S(2)}) collective-permute-start(f32[2,64,4096]{2,1,0:T(8,128)} %collective-permute-done.9.refs_6_), channel_id=1, source_target_pairs={{1,0},{0,1},{3,2},{2,3},{5,4},{4,5},{7,6},{6,7},{9,8},{8,9},{11,10... | collective-permute-start | bytes 6291464 | tf_op jit(solution)/shard_map/ppermute | solution.py:28
  95.5 6.4 %collective-permute-start.3 = (s32[1,8]{1,0:T(1,128)S(1)}, s32[1,8]{1,0:T(1,128)S(1)}, u32[]{:S(2)}, u32[]{:S(2)}) collective-permute-start(s32[1,8]{1,0:T(1,128)S(1)} %pad_add_fusion.1), channel_id=1, source_target_pairs={{29,0},{4,1},{31,2},{6,3},{1,4},{8,5},{3,6},{10,7},{5,8},{12,9},{7... | collective-permute-start | bytes 104 | tf_op jit(solution)/shard_map/ppermute | solution.py:28
  97.2 6.5 %collective-permute-start.2 = (s32[1,8]{1,0:T(1,128)S(1)}, s32[1,8]{1,0:T(1,128)S(1)}, u32[]{:S(2)}, u32[]{:S(2)}) collective-permute-start(s32[1,8]{1,0:T(1,128)S(1)} %pad_add_fusion.1), channel_id=1, source_target_pairs={{30,0},{3,1},{0,2},{5,3},{2,4},{7,5},{4,6},{9,7},{6,8},{11,9},{8,1... | collective-permute-start | bytes 104 | tf_op jit(solution)/shard_map/ppermute | solution.py:28
  101.9 5.5 %collective-permute-start.1 = (s32[1,8]{1,0:T(1,128)S(1)}, s32[1,8]{1,0:T(1,128)S(1)}, u32[]{:S(2)}, u32[]{:S(2)}) collective-permute-start(s32[1,8]{1,0:T(1,128)S(1)} %pad_add_fusion.1), channel_id=1, source_target_pairs={{31,0},{2,1},{1,2},{4,3},{3,4},{6,5},{5,6},{8,7},{7,8},{10,9},{9,1... | collective-permute-start | bytes 104 | tf_op jit(solution)/shard_map/ppermute | solution.py:28
  103.7 4.5 %collective-permute-start = (s32[1,8]{1,0:T(1,128)S(1)}, s32[1,8]{1,0:T(1,128)S(1)}, u32[]{:S(2)}, u32[]{:S(2)}) collective-permute-start(s32[1,8]{1,0:T(1,128)S(1)} %pad_add_fusion.1), channel_id=1, source_target_pairs={{1,0},{0,1},{3,2},{2,3},{5,4},{4,5},{7,6},{6,7},{9,8},{8,9},{11,10... | collective-permute-start | bytes 104 | tf_op jit(solution)/shard_map/ppermute | solution.py:28
  115.3 31.3 %collective-permute-start.11 = (f32[32,64,128]{2,1,0:T(8,128)}, f32[32,64,128]{2,1,0:T(8,128)S(1)}, u32[]{:S(2)}, u32[]{:S(2)}) collective-permute-start(f32[32,64,128]{2,1,0:T(8,128)} %get-tuple-element.12), channel_id=1, source_target_pairs={{29,0},{4,1},{31,2},{6,3},{1,4},{8,5},{3,6},{10,7},{5,8},{12,9},{7... | collective-permute-start | bytes 3145736 | tf_op jit(solution)/shard_map/ppermute | solution.py:28
  115.3 44.5 %collective-permute-start.6 = (f32[32,32,128]{2,1,0:T(8,128)}, f32[32,32,128]{2,1,0:T(8,128)}, u32[]{:S(2)}, u32[]{:S(2)}) collective-permute-start(f32[32,32,128]{2,1,0:T(8,128)} %get-tuple-element.10), channel_id=1, source_target_pairs={{4,0},{29,1},{6,2},{31,3},{8,4},{1,5},{10,6},{3,7},{12,8},{5,9},{1... | collective-permute-start | bytes 1572872 | tf_op jit(solution)/shard_map/ppermute | solution.py:28
  115.4 2.2 %collective-permute-start.4 = (s32[2,8]{1,0:T(2,128)S(1)}, s32[2,8]{1,0:T(2,128)S(1)}, u32[]{:S(2)}, u32[]{:S(2)}) collective-permute-start(s32[2,8]{1,0:T(2,128)S(1)} %pad_add_fusion), channel_id=1, source_target_pairs={{1,0},{0,1},{3,2},{2,3},{5,4},{4,5},{7,6},{6,7},{9,8},{8,9},{11,10... | collective-permute-start | bytes 200 | tf_op jit(solution)/shard_map/ppermute | solution.py:28
  146.6 1.1 copy-start.1
